TPU v7x, 32 devices: a whole 2x2x4 slice. The times are simulated.
32 devices in a mesh: dp: 4 (over y, core), expert: 8 (over z, x).
Axes of the slice: x: 2, y: 2, z: 4, core: 2. Of those that a mesh axis runs over, the one named last changes fastest.
Arguments:
- tokens: bfloat16 [32768, 768], P(('dp', 'expert')), may hold values from -6 to 6
- lengths: int32 [32], P(('dp', 'expert')), may hold values from 144 to 1024, as said below
- routes: int32 [32768], P(('dp', 'expert')), may hold values from 0 to 7, as said below
- attn_in: bfloat16 [2304, 768], P(('dp', 'expert')), may hold values from -0.21875 to 0.21875
- attn_out: bfloat16 [768, 768], P(('dp', 'expert')), may hold values from -3.5 to 3.5
- ln_gain: bfloat16 [2, 768], P(None, ('dp', 'expert')), may hold values from 0.25 to 1.75
- ln_bias: bfloat16 [2, 768], P(None, ('dp', 'expert')), may hold values from -1.1953125 to 1.1953125
- w_in: bfloat16 [8, 768, 3072], P('expert', None, 'dp'), may hold values from -0.21875 to 0.21875
- w_out: bfloat16 [8, 3072, 768], P('expert', 'dp'), may hold values from -0.109375 to 0.109375
- cotangent: bfloat16 [32768, 768], P(('dp', 'expert')), may hold values from -6 to 6
Outputs:
- block_out: bfloat16 [32768, 768], P(('dp', 'expert'))
- grad_tokens: float32 [32768, 768], P(('dp', 'expert'))
- grad_attn_in: float32 [2304, 768], P(('dp', 'expert'))
- grad_attn_out: float32 [768, 768], P(('dp', 'expert'))
- grad_gain: float32 [2, 768], P(None, ('dp', 'expert'))
- grad_bias: float32 [768], P(('dp', 'expert'))
- grad_bias_moe: float32 [768], P(('dp', 'expert'))
- grad_w_in: float32 [8, 768, 3072], P('expert', None, 'dp')
- grad_w_out: float32 [8, 3072, 768], P('expert', 'dp')
Inputs may be any that keep to these rules, and one draw needn't show every extreme that they name: `lengths`: every draw has a sequence of the full 1024 positions. `routes`: among the valid tokens of one sequence, at most 144 name the same expert; in every draw some expert receives exactly 144 valid tokens from every sequence of some index of dp.
All inputs are finite; a program needn't handle non-finite values.
Results may differ from a plain program's by a relative error of at most 0.012.
Values may be sent and summed in bfloat16 or wider, within the bound.
No kernel may reach another device: no remote copies, remote signals or barrier semaphores. Data moves between devices by JAX's collectives and lax.ppermute only.
A program may use at most 256 MiB of HBM per device.

v0:
```python
import jax
import jax.numpy as jnp
from jax import lax
from jax.sharding import PartitionSpec as P

HEADS = 12
HEAD_DIM = 64
eps = 1e-05
masked_score = -1e30


def product(left, right):
    return jnp.dot(left, right, preferred_element_type=jnp.float32)


def contract(left, right, left_dim, right_dim):
    return lax.dot_general(
        left, right, (((left_dim,), (right_dim,)), ((), ())), preferred_element_type=jnp.float32
    )


def layer_norm(values, gain, shift):
    centre = jnp.mean(values, axis=-1, keepdims=True)
    centred = values - centre
    spread = jnp.mean(centred * centred, axis=-1, keepdims=True)
    return centred * lax.rsqrt(spread + eps) * gain + shift


def gelu_exact(values):
    return jax.nn.gelu(values, approximate=False)


def gelu_grad(pre, grad_act):
    unused, pull = jax.vjp(gelu_exact, pre)
    return pull(grad_act)[0]


def block_scores(query_rows, key_rows, first_row, last_row, limit):
    query_pos = jnp.arange(first_row, last_row)[:, None]
    key_pos = jnp.arange(last_row)[None, :]
    allowed = (key_pos <= query_pos) & (key_pos < limit)
    scores = jnp.einsum(
        "qhd,khd->hqk", query_rows, key_rows, preferred_element_type=jnp.float32
    ) * HEAD_DIM ** (-0.5)
    return jnp.where(allowed[None], scores, masked_score)


def shards(tokens, lengths, routes, attn_in, attn_out, ln_gain, ln_bias, w_in, w_out, cotangent):
    row_count, model_width = tokens.shape
    shaped = (row_count, HEADS, HEAD_DIM)
    scale = HEAD_DIM ** (-0.5)
    limit = lengths[0]
    all_in, all_out, gains, shifts = (
        lax.all_gather(attn_in, ("dp", "expert"), axis=0, tiled=True),
        lax.all_gather(attn_out, ("dp", "expert"), axis=0, tiled=True),
        lax.all_gather(ln_gain, ("dp", "expert"), axis=1, tiled=True),
        lax.all_gather(ln_bias, ("dp", "expert"), axis=1, tiled=True),
    )
    gains = gains.astype(jnp.float32)
    shifts = shifts.astype(jnp.float32)
    w_query = all_in[:model_width]
    w_key = all_in[model_width : 2 * model_width]
    w_value = all_in[2 * model_width :]
    resid = tokens.astype(jnp.float32)
    normed_low = layer_norm(resid, gains[0], shifts[0]).astype(jnp.bfloat16)
    query = product(normed_low, w_query).astype(jnp.bfloat16).reshape(shaped)
    key_rows = product(normed_low, w_key).astype(jnp.bfloat16).reshape(shaped)
    value_rows = product(normed_low, w_value).astype(jnp.bfloat16).reshape(shaped)
    block = min(512, row_count)
    block_count = row_count // block
    mixed_parts = []
    log_totals = []
    for number in range(block_count):
        first_row = number * block
        last_row = first_row + block
        scores = block_scores(
            query[first_row:last_row], key_rows[:last_row], first_row, last_row, limit
        )
        top_score = jnp.max(scores, axis=-1, keepdims=True)
        weights = jnp.exp(scores - top_score)
        totals = jnp.sum(weights, axis=-1, keepdims=True)
        probs_low = (weights / totals).astype(jnp.bfloat16)
        log_totals.append(top_score + jnp.log(totals))
        mixed_parts.append(
            jnp.einsum(
                "hqk,khd->qhd", probs_low, value_rows[:last_row], preferred_element_type=jnp.float32
            ).astype(jnp.bfloat16)
        )
    mixed_low = jnp.concatenate(mixed_parts, axis=0).reshape(row_count, model_width)
    hidden = resid + product(mixed_low, all_out)
    moe_in = layer_norm(hidden, gains[1], shifts[1]).astype(jnp.bfloat16)
    experts = lax.axis_size("expert")
    capacity = max(2, 9 * row_count // (8 * experts))
    slot_total = experts * capacity
    valid = jnp.arange(row_count) < limit
    onehot = ((routes[:, None] == jnp.arange(experts)[None, :]) & valid[:, None]).astype(jnp.int32)
    ranks = jnp.sum((jnp.cumsum(onehot, axis=0) - 1) * onehot, axis=1)
    target = jnp.where(valid, routes * capacity + ranks, slot_total)
    fetch_at = jnp.minimum(target, slot_total - 1)
    send_rows = (
        jnp.zeros((slot_total, model_width), jnp.bfloat16).at[target].set(moe_in, mode="drop")
    )
    received = lax.all_to_all(
        send_rows.reshape(experts, capacity, model_width),
        "expert",
        split_axis=0,
        concat_axis=0,
        tiled=True,
    )
    full_in, full_out = (
        lax.all_gather(w_in, "dp", axis=2, tiled=True),
        lax.all_gather(w_out, "dp", axis=1, tiled=True),
    )
    flat_rows = received.reshape(-1, model_width)
    pre = product(flat_rows, full_in[0])
    act_low = gelu_exact(pre).astype(jnp.bfloat16)
    result = (
        product(act_low, full_out[0]).astype(jnp.bfloat16).reshape(experts, capacity, model_width)
    )
    returned = lax.all_to_all(result, "expert", split_axis=0, concat_axis=0, tiled=True)
    back_rows = returned.reshape(-1, model_width)[fetch_at]
    expert_term = jnp.where(valid[:, None], back_rows.astype(jnp.float32), 0.0)
    block_out = (hidden + expert_term).astype(jnp.bfloat16)
    grad_slots = (
        jnp.zeros((slot_total, model_width), jnp.bfloat16).at[target].set(cotangent, mode="drop")
    )
    grad_recv = lax.all_to_all(
        grad_slots.reshape(experts, capacity, model_width),
        "expert",
        split_axis=0,
        concat_axis=0,
        tiled=True,
    )
    grad_flat = grad_recv.reshape(-1, model_width)
    grad_act = contract(grad_flat, full_out[0], 1, 1)
    grad_pre = gelu_grad(pre, grad_act).astype(jnp.bfloat16)
    term_out = contract(act_low, grad_flat, 0, 0)
    term_in = contract(flat_rows, grad_pre, 0, 0)
    grad_moe = (
        contract(grad_pre, full_in[0], 1, 1)
        .astype(jnp.bfloat16)
        .reshape(experts, capacity, model_width)
    )
    grad_w_in, grad_w_out = (
        lax.psum_scatter(
            term_in[None].astype(jnp.bfloat16), "dp", scatter_dimension=2, tiled=True
        ).astype(jnp.float32),
        lax.psum_scatter(
            term_out[None].astype(jnp.bfloat16), "dp", scatter_dimension=1, tiled=True
        ).astype(jnp.float32),
    )
    grad_back = lax.all_to_all(grad_moe, "expert", split_axis=0, concat_axis=0, tiled=True)
    grad_moe_in = jnp.where(
        valid[:, None], grad_back.reshape(-1, model_width)[fetch_at].astype(jnp.float32), 0.0
    )
    unused, pull_second = jax.vjp(layer_norm, hidden, gains[1], shifts[1])
    grad_from_norm, gain_second, shift_second = pull_second(grad_moe_in)
    grad_hidden = cotangent.astype(jnp.float32) + grad_from_norm
    grad_hidden_low = grad_hidden.astype(jnp.bfloat16)
    grad_attn_out = contract(mixed_low, grad_hidden_low, 0, 0)
    grad_mixed = contract(grad_hidden_low, all_out, 1, 1).astype(jnp.bfloat16).reshape(shaped)
    grad_key_sum = jnp.zeros(shaped, jnp.float32)
    grad_value_sum = jnp.zeros(shaped, jnp.float32)
    grad_query_parts = []
    for number in range(block_count):
        first_row = number * block
        last_row = first_row + block
        query_block = query[first_row:last_row]
        scores = block_scores(query_block, key_rows[:last_row], first_row, last_row, limit)
        probs = jnp.exp(scores - log_totals[number])
        probs_low = probs.astype(jnp.bfloat16)
        grad_block = grad_mixed[first_row:last_row]
        grad_probs = jnp.einsum(
            "qhd,khd->hqk", grad_block, value_rows[:last_row], preferred_element_type=jnp.float32
        )
        grad_scores = probs * (grad_probs - jnp.sum(probs * grad_probs, axis=-1, keepdims=True))
        grad_scores_low = grad_scores.astype(jnp.bfloat16)
        grad_query_parts.append(
            jnp.einsum(
                "hqk,khd->qhd",
                grad_scores_low,
                key_rows[:last_row],
                preferred_element_type=jnp.float32,
            )
            * scale
        )
        grad_key_sum = grad_key_sum.at[:last_row].add(
            jnp.einsum(
                "hqk,qhd->khd", grad_scores_low, query_block, preferred_element_type=jnp.float32
            )
            * scale
        )
        grad_value_sum = grad_value_sum.at[:last_row].add(
            jnp.einsum("hqk,qhd->khd", probs_low, grad_block, preferred_element_type=jnp.float32)
        )
    grad_query = (
        jnp.concatenate(grad_query_parts, axis=0)
        .astype(jnp.bfloat16)
        .reshape(row_count, model_width)
    )
    grad_key = grad_key_sum.astype(jnp.bfloat16).reshape(row_count, model_width)
    grad_value = grad_value_sum.astype(jnp.bfloat16).reshape(row_count, model_width)
    grad_attn_in = jnp.concatenate(
        [
            contract(normed_low, grad_query, 0, 0),
            contract(normed_low, grad_key, 0, 0),
            contract(normed_low, grad_value, 0, 0),
        ],
        axis=0,
    )
    grad_normed = (
        contract(grad_query, w_query, 1, 1)
        + contract(grad_key, w_key, 1, 1)
        + contract(grad_value, w_value, 1, 1)
    )
    unused, pull_first = jax.vjp(layer_norm, resid, gains[0], shifts[0])
    grad_from_first, gain_first, shift_first = pull_first(grad_normed)
    grad_tokens = grad_hidden + grad_from_first
    gain_terms = jnp.stack([gain_first, gain_second], axis=0)
    shift_terms = jnp.stack([shift_first, shift_second], axis=0)
    grad_attn_in, grad_attn_out, grad_gain, shift_sums = (
        lax.psum_scatter(grad_attn_in, ("dp", "expert"), scatter_dimension=0, tiled=True),
        lax.psum_scatter(grad_attn_out, ("dp", "expert"), scatter_dimension=0, tiled=True),
        lax.psum_scatter(gain_terms, ("dp", "expert"), scatter_dimension=1, tiled=True),
        lax.psum_scatter(shift_terms, ("dp", "expert"), scatter_dimension=1, tiled=True),
    )
    return (
        block_out,
        grad_tokens,
        grad_attn_in,
        grad_attn_out,
        grad_gain,
        shift_sums[0],
        shift_sums[1],
        grad_w_in,
        grad_w_out,
    )


def solution(mesh):
    in_specs = (
        P(("dp", "expert"), None),
        P(("dp", "expert")),
        P(("dp", "expert")),
        P(("dp", "expert"), None),
        P(("dp", "expert"), None),
        P(None, ("dp", "expert")),
        P(None, ("dp", "expert")),
        P("expert", None, "dp"),
        P("expert", "dp", None),
        P(("dp", "expert"), None),
    )
    out_specs = (
        P(("dp", "expert"), None),
        P(("dp", "expert"), None),
        P(("dp", "expert"), None),
        P(("dp", "expert"), None),
        P(None, ("dp", "expert")),
        P(("dp", "expert")),
        P(("dp", "expert")),
        P("expert", None, "dp"),
        P("expert", "dp", None),
    )
    return jax.shard_map(shards, mesh=mesh, in_specs=in_specs, out_specs=out_specs, check_vma=False)
```

profile of v0, /device:TPU:0, one launch (start us, length us, event | category | flops | bytes accessed | tf_op | source)
XLA Modules:
  0.0 758.8 jit_solution(4380178754818980319)
XLA Ops:
  10.1 69.6 %all-gather = bf16[32,24,2]{1,2,0:T(2,128)(2,1)S(1)} all-gather(bf16[1,24,2]{1,2,0:T(2,128)(2,1)} %bitcast.183), channel_id=1, replica_groups=mesh['dp'=4,'expert'=8] {'dp','expert'}, dimensions={0}, use_global_device_ids=true | all-gather | bytes 3168 | tf_op jit(solution)/shard_map/all_gather | solution.py:56
  79.7 63.2 %all-gather.1 = bf16[32,24,2]{1,2,0:T(2,128)(2,1)S(1)} all-gather(bf16[1,24,2]{1,2,0:T(2,128)(2,1)} %bitcast.184), channel_id=1, replica_groups=mesh['dp'=4,'expert'=8] {'dp','expert'}, dimensions={0}, use_global_device_ids=true | all-gather | bytes 3168 | tf_op jit(solution)/shard_map/all_gather | solution.py:57
  159.7 10.8 %fusion.14 = (f32[12,512]{1,0:T(8,128)S(1)}, f32[12,512,1024]{2,1,0:T(8,128)}) fusion(pred[512,1024]{1,0:T(8,128)(4,1)S(1)} %fusion.50, bf16[512,12,64]{0,2,1:T(8,128)(2,1)S(1)} %bitcast.154, bf16[1024,12,64]{0,2,1:T(8,128)(2,1)S(1)} %bitcast.152), kind=kOutput, calls=%fused_computation.40 | convolution fusion | flops 824174592 | bytes 28073984 | tf_op jit(solution)/shard_map/qhd,khd->hqk/dot_general | solution.py:42
  170.5 12.3 %fusion = f32[12,512]{1,0:T(8,128)S(1)} fusion(f32[12,512]{1,0:T(8,128)S(1)} %get-tuple-element.135, f32[12,512,1024]{2,1,0:T(8,128)} %get-tuple-element.136, pred[512,1024]{1,0:T(8,128)(4,1)S(1)} %fusion.50), kind=kLoop, calls=%fused_computation.10 | loop fusion | flops 25159680 | bytes 25739264 | tf_op jit(solution)/shard_map/reduce_sum | solution.py:81
  186.5 8.8 %fusion.59 = bf16[512,12,64]{0,2,1:T(8,128)(2,1)} fusion(bf16[1024,12,64]{0,2,1:T(8,128)(2,1)S(1)} %bitcast.158, f32[12,512]{1,0:T(8,128)S(1)} %fusion, f32[12,512]{1,0:T(8,128)S(1)} %get-tuple-element.135, f32[12,512,1024]{2,1,0:T(8,128)S(1)} %copy-done, pred[512,1024]{1,0:T(8,128)(4,1)S(1)} %fusion.50), kind=kOutput, calls=%fused_computation.105 | convolution fusion | flops 837156864 | bytes 28098560 | tf_op jit(solution)/shard_map/hqk,khd->qhd/dot_general | solution.py:85
  225.1 7.1 scatter_custom_fusion.1
  232.3 31.8 %all-to-all-done = bf16[8,144,768]{2,1,0:T(8,128)(2,1)S(1)} async-done(((bf16[8,144,768]{2,1,0:T(8,128)(2,1)}), bf16[8,144,768]{2,1,0:T(8,128)(2,1)S(1)}, u32[]{:S(2)}, u32[]{:S(2)}) %all-to-all-start) | async-done | bytes 1769504 | tf_op jit(solution)/shard_map/all_to_all | solution.py:103
  268.5 48.2 %multiply_convert_fusion.1 = (bf16[1152,3072]{1,0:T(8,128)(2,1)}, f32[1152,3072]{1,0:T(8,128)}, f32[1152,3072]{1,0:T(8,128)}) fusion(bf16[1152,768]{1,0:T(8,128)(2,1)S(1)} %bitcast.170, bf16[1,768,3072]{2,1,0:T(8,128)(2,1)} %all-gather.11.cloned.1.call-done), kind=kOutput, calls=%fused_computation.15 | convolution fusion | flops 5665849344 | bytes 41877504 | tf_op jit(solution)/shard_map/dot_general | solution.py:13
  316.7 10.6 %fusion.31 = bf16[1,3072,768]{2,1,0:T(8,128)(2,1)} fusion(bf16[1152,3072]{1,0:T(8,128)(2,1)} %get-tuple-element.123, bf16[1152,768]{1,0:T(8,128)(2,1)} %bitcast.25), kind=kOutput, calls=%fused_computation.64 | convolution fusion | flops 5438177280 | bytes 13565952 | tf_op jit(solution)/shard_map/dot_general | solution.py:17
  327.3 20.0 %add_convert_fusion = bf16[1152,3072]{1,0:T(8,128)(2,1)} fusion(f32[1152,3072]{1,0:T(8,128)} %get-tuple-element.124, bf16[1152,768]{1,0:T(8,128)(2,1)} %bitcast.25, f32[1152,3072]{1,0:T(8,128)} %get-tuple-element.141, bf16[1,3072,768]{2,1,0:T(8,128)(2,1)} %all-gather.13.cloned.1.call-done), kind=kOutput, calls=%fused_computation.14 | convolution fusion | flops 5485363200 | bytes 41877504 | tf_op jit(solution)/shard_map/dot_general | solution.py:17
  347.4 10.8 %fusion.35 = bf16[1152,768]{1,0:T(8,128)(2,1)} fusion(bf16[1152,3072]{1,0:T(8,128)(2,1)} %add_convert_fusion, bf16[1,768,3072]{2,1,0:T(8,128)(2,1)} %all-gather.11.cloned.1.call-done), kind=kOutput, calls=%fused_computation.68 | convolution fusion | flops 5436702720 | bytes 13565952 | tf_op jit(solution)/shard_map/dot_general | solution.py:17
  369.5 11.0 %fusion.30 = bf16[1,768,3072]{2,1,0:T(8,128)(2,1)} fusion(bf16[1152,768]{1,0:T(8,128)(2,1)S(1)} %bitcast.171, bf16[1152,3072]{1,0:T(8,128)(2,1)} %add_convert_fusion), kind=kOutput, calls=%fused_computation.63 | convolution fusion | flops 5438177280 | bytes 13565952 | tf_op jit(solution)/shard_map/dot_general | solution.py:17
  380.6 23.5 %all-to-all-done.3 = bf16[8,144,768]{2,1,0:T(8,128)(2,1)S(1)} async-done(((bf16[8,144,768]{2,1,0:T(8,128)(2,1)}), bf16[8,144,768]{2,1,0:T(8,128)(2,1)S(1)}, u32[]{:S(2)}, u32[]{:S(2)}) %all-to-all-start.3) | async-done | bytes 1769504 | tf_op jit(solution)/shard_map/all_to_all | solution.py:152
  425.7 10.9 %multiply_reduce_fusion.1 = (f32[12,512]{1,0:T(8,128)S(1)}, f32[12,512,512]{1,2,0:T(8,128)}) fusion(f32[12,512]{1,0:T(8,128)S(1)} %copy-done.47, f32[12,512,512]{1,2,0:T(8,128)} %copy-done.1, pred[512,512]{0,1:T(8,128)(4,1)S(1)} %copy-done.24, bf16[512,12,64]{0,2,1:T(8,128)(2,1)S(1)} %bitcast.162, bf16[512,12,64]{0,2,1:T(8,128)(2,1)S(1)} %bitcast.161), kind=kOutput, calls=%fused_computation.32 | convolution fusion | flops 418375680 | bytes 27049984 | tf_op jit(solution)/shard_map/qhd,khd->hqk/dot_general | solution.py:173
  436.9 7.0 multiply_convert_fusion.2
  447.1 21.5 %multiply_reduce_fusion = (f32[12,512]{1,0:T(8,128)S(1)}, f32[12,512,1024]{2,1,0:T(8,128)}) fusion(f32[12,512]{1,0:T(8,128)S(1)} %copy-done.46, f32[12,512,1024]{2,1,0:T(8,128)} %get-tuple-element.136, pred[512,1024]{1,0:T(8,128)(4,1)S(1)} %copy-done.15, bf16[512,12,64]{0,2,1:T(8,128)(2,1)S(1)} %bitcast.164, bf16[1024,12,64]{0,2,1:T(8,128)(2,1)S(1)} %bitcast.159), kind=kOutput, calls=%fused_computation.5 | convolution fusion | flops 836757504 | bytes 53264384 | tf_op jit(solution)/shard_map/qhd,khd->hqk/dot_general | solution.py:173
  468.6 17.2 %multiply_convert_fusion = bf16[12,512,1024]{2,1,0:T(8,128)(2,1)S(1)} fusion(f32[12,512,1024]{2,1,0:T(8,128)} %get-tuple-element.143, f32[12,512]{1,0:T(8,128)S(1)} %get-tuple-element.142, f32[12,512]{1,0:T(8,128)S(1)} %copy-done.46, f32[12,512,1024]{2,1,0:T(8,128)} %get-tuple-element.136, pred[512,1024]{1,0:T(8,128)(4,1)} %copy-done.14), kind=kLoop, calls=%fused_computation.4 | loop fusion | flops 37748736 | bytes 63488000 | tf_op jit(solution)/shard_map/convert_element_type | solution.py:177
  485.8 7.5 multiply_convert_fusion.3
  493.3 9.1 %fusion.54 = f32[512,12,64]{0,2,1:T(8,128)} fusion(bf16[512,12,64]{0,2,1:T(8,128)(2,1)} %bitcast.163, f32[12,512]{1,0:T(8,128)S(1)} %copy-done.47, f32[12,512,512]{1,2,0:T(8,128)} %copy-done.1, pred[512,512]{0,1:T(8,128)(4,1)S(1)} %copy-done.24), kind=kOutput, calls=%fused_computation.102 | convolution fusion | flops 415236096 | bytes 15228928 | tf_op jit(solution)/shard_map/hqk,qhd->khd/dot_general | solution.py:194
  502.5 13.5 %fusion.46 = bf16[1024,12,64]{0,2,1:T(8,128)(2,1)} fusion(f32[512,12,64]{0,2,1:T(8,128)} %fusion.54, bf16[512,12,64]{0,2,1:T(8,128)(2,1)S(1)} %bitcast.165, f32[12,512]{1,0:T(8,128)S(1)} %copy-done.46, f32[12,512,1024]{2,1,0:T(8,128)} %get-tuple-element.136, pred[512,1024]{1,0:T(8,128)(4,1)S(1)} %copy-done.16), kind=kOutput, calls=%fused_computation.76 | convolution fusion | flops 832045056 | bytes 29646848 | tf_op jit(solution)/shard_map/hqk,qhd->khd/dot_general | solution.py:194
  533.2 10.3 %fusion.38 = bf16[1152,768]{1,0:T(8,128)(2,1)} fusion(bf16[1152,3072]{1,0:T(8,128)(2,1)} %get-tuple-element.123, bf16[1,3072,768]{2,1,0:T(8,128)(2,1)} %all-gather.13.cloned.1.call-done), kind=kOutput, calls=%fused_computation.69 | convolution fusion | flops 5436702720 | bytes 13565952 | tf_op jit(solution)/shard_map/dot_general | solution.py:13
  547.1 47.3 %all-to-all-done.1 = bf16[8,144,768]{2,1,0:T(8,128)(2,1)S(1)} async-done(((bf16[8,144,768]{2,1,0:T(8,128)(2,1)}), bf16[8,144,768]{2,1,0:T(8,128)(2,1)S(1)}, u32[]{:S(2)}, u32[]{:S(2)}) %all-to-all-start.1) | async-done | bytes 1769504 | tf_op jit(solution)/shard_map/all_to_all | solution.py:120
  617.9 38.2 %all-reduce.4 = (f32[2,768]{1,0:T(2,128)S(1)}, f32[2,768]{1,0:T(2,128)S(1)}) all-reduce(f32[2,768]{1,0:T(2,128)S(1)} %pad_maximum_fusion.5, f32[2,768]{1,0:T(2,128)S(1)} %pad_maximum_fusion.6), channel_id=4, replica_groups=mesh['dp'=4,'expert'=8] {'dp','expert'}, use_global_device_ids=true, to_apply=%region_23.24.clone | all-reduce | flops 3072 | bytes 24576
  663.1 88.4 %reduce-scatter.7.cloned.1.call-done = f32[72,768]{1,0:T(8,128)} async-done(((f32[2304,768]{1,0:T(8,128)}), f32[72,768]{1,0:T(8,128)}) %reduce-scatter.7.cloned.1.call-update) | async-done | bytes 221200 | tf_op jit(solution)/shard_map/reduce_scatter | solution.py:222
  (277 shorter events, 144.0 us)
Async XLA Ops:
  7.2 144.9 %all-gather.7.cloned.1.call-start = ((), (), s32[]{:S(2)}) async-start(), calls=%async_computation.8 | async-start | bytes 3649536 | tf_op jit(solution)/shard_map/all_gather | solution.py:54
  7.9 200.3 %all-gather.9.cloned.1.call-start = ((), (), s32[]{:S(2)}) async-start(), calls=%async_computation.9 | async-start | bytes 1216512 | tf_op jit(solution)/shard_map/all_gather | solution.py:55
  8.7 259.8 %all-gather.11.cloned.1.call-start = ((), (), s32[]{:S(2)}) async-start(), calls=%async_computation.10 | async-start | bytes 5898240 | tf_op jit(solution)/shard_map/all_gather | solution.py:111
  10.1 137.7 %copy-start.67 = (pred[1024]{0:T(1024)(128)(4,1)}, pred[1024]{0:T(1024)(128)(4,1)S(1)}, u32[]{:S(2)}) copy-start(pred[1024]{0:T(1024)(128)(4,1)S(1)} %iota_compare_fusion.4) | copy-start | bytes 3076
  147.0 55.9 %copy-start.23 = (pred[512,512]{0,1:T(8,128)(4,1)}, pred[512,512]{0,1:T(8,128)(4,1)S(1)}, u32[]{:S(2)}) copy-start(pred[512,512]{0,1:T(8,128)(4,1)S(1)} %fusion.61) | copy-start | bytes 786436
  148.1 38.3 %copy-start.14 = (pred[512,1024]{1,0:T(8,128)(4,1)}, pred[512,1024]{1,0:T(8,128)(4,1)S(1)}, u32[]{:S(2)}) copy-start(pred[512,1024]{1,0:T(8,128)(4,1)S(1)} %fusion.50) | copy-start | bytes 1572868
  150.1 58.2 %copy-start.7 = (bf16[1024,768]{0,1:T(8,128)(2,1)}, bf16[1024,768]{0,1:T(8,128)(2,1)S(1)}, u32[]{:S(2)}) copy-start(bf16[1024,768]{0,1:T(8,128)(2,1)S(1)} %copy.64) | copy-start | bytes 4718596
  150.4 32.4 %copy-start.54 = (f32[1024]{0:T(1024)}, f32[1024]{0:T(1024)S(1)}, u32[]{:S(2)}) copy-start(f32[1024]{0:T(1024)S(1)} %broadcast_multiply_fusion.1) | copy-start | bytes 12292
  150.9 31.9 %copy-start.65 = (f32[1024]{0:T(1024)}, f32[1024]{0:T(1024)S(1)}, u32[]{:S(2)}) copy-start(f32[1024]{0:T(1024)S(1)} %fusion.82) | copy-start | bytes 12292
  151.5 31.3 %copy-start.58 = (f32[768]{0:T(1024)}, f32[768]{0:T(1024)S(1)}, u32[]{:S(2)}) copy-start(f32[768]{0:T(1024)S(1)} %get-tuple-element.147) | copy-start | bytes 9220
  151.5 31.3 %copy-start.70 = (f32[768]{0:T(1024)}, f32[768]{0:T(1024)S(1)}, u32[]{:S(2)}) copy-start(f32[768]{0:T(1024)S(1)} %get-tuple-element.120) | copy-start | bytes 9220
  151.5 60.5 %copy-start.50 = (f32[768]{0:T(1024)}, f32[768]{0:T(1024)S(1)}, u32[]{:S(2)}) copy-start(f32[768]{0:T(1024)S(1)} %get-tuple-element.148) | copy-start | bytes 9220
  155.1 40.2 %copy-start.17 = (bf16[512,768]{0,1:T(8,128)(2,1)}, bf16[512,768]{0,1:T(8,128)(2,1)S(1)}, u32[]{:S(2)}) copy-start(bf16[512,768]{0,1:T(8,128)(2,1)S(1)} %slice.190) | copy-start | bytes 2359300
  221.0 43.1 %all-to-all-start = ((bf16[8,144,768]{2,1,0:T(8,128)(2,1)}), bf16[8,144,768]{2,1,0:T(8,128)(2,1)S(1)}, u32[]{:S(2)}, u32[]{:S(2)}) async-start(bf16[8,144,768]{2,1,0:T(8,128)(2,1)} %bitcast.18), calls=%async_computation | async-start | bytes 3538944 | tf_op jit(solution)/shard_map/all_to_all | solution.py:103
  224.6 102.8 %all-gather.13.cloned.1.call-start = ((), (), s32[]{:S(2)}) async-start(), calls=%async_computation.11 | async-start | bytes 5898240 | tf_op jit(solution)/shard_map/all_gather | solution.py:112
  264.1 52.6 %all-to-all-start.2 = ((bf16[8,144,768]{2,1,0:T(8,128)(2,1)}), bf16[8,144,768]{2,1,0:T(8,128)(2,1)}, u32[]{:S(2)}, u32[]{:S(2)}) async-start(bf16[8,144,768]{2,1,0:T(8,128)(2,1)} %bitcast.24), calls=%async_computation.2 | async-start | bytes 3538944 | tf_op jit(solution)/shard_map/all_to_all | solution.py:127
  268.4 388.9 %reduce-scatter.13.cloned.1.call-start = ((), (), s32[]{:S(2)}) async-start(), calls=%async_computation.15 | async-start | bytes 5898240 | tf_op jit(solution)/shard_map/reduce_scatter | solution.py:148
  358.2 45.9 %all-to-all-start.3 = ((bf16[8,144,768]{2,1,0:T(8,128)(2,1)}), bf16[8,144,768]{2,1,0:T(8,128)(2,1)S(1)}, u32[]{:S(2)}, u32[]{:S(2)}) async-start(bf16[8,144,768]{2,1,0:T(8,128)(2,1)} %bitcast.172), calls=%async_computation.3 | async-start | bytes 3538944 | tf_op jit(solution)/shard_map/all_to_all | solution.py:152
  364.1 296.2 %reduce-scatter.11.cloned.1.call-start = ((), (), s32[]{:S(2)}) async-start(), calls=%async_computation.14 | async-start | bytes 5898240 | tf_op jit(solution)/shard_map/reduce_scatter | solution.py:145
  380.5 23.6 %copy-start.69 = (s32[1024]{0:T(1024)S(1)}, s32[1024]{0:T(1024)}, u32[]{:S(2)}) copy-start(s32[1024]{0:T(1024)} %get-tuple-element.131) | copy-start | bytes 12292
  380.5 282.6 %reduce-scatter.9.cloned.1.call-start = ((), (), s32[]{:S(2)}) async-start(), calls=%async_computation.13 | async-start | bytes 2433024 | tf_op jit(solution)/shard_map/reduce_scatter | solution.py:223
  424.2 22.9 %copy-start.31 = (bf16[512,768]{0,1:T(8,128)(2,1)}, bf16[512,768]{0,1:T(8,128)(2,1)S(1)}, u32[]{:S(2)}) copy-start(bf16[512,768]{0,1:T(8,128)(2,1)S(1)} %get-tuple-element.128) | copy-start | bytes 2359300
  516.0 235.5 %reduce-scatter.7.cloned.1.call-start = ((), (), s32[]{:S(2)}) async-start(), calls=%async_computation.12 | async-start | bytes 7299072 | tf_op jit(solution)/shard_map/reduce_scatter | solution.py:222
  543.5 50.9 %all-to-all-start.1 = ((bf16[8,144,768]{2,1,0:T(8,128)(2,1)}), bf16[8,144,768]{2,1,0:T(8,128)(2,1)S(1)}, u32[]{:S(2)}, u32[]{:S(2)}) async-start(bf16[8,144,768]{2,1,0:T(8,128)(2,1)} %bitcast.22), calls=%async_computation.1 | async-start | bytes 3538944 | tf_op jit(solution)/shard_map/all_to_all | solution.py:120
  (69 other events, 353.9 us)
Sparse Core Ops, SparseCore 0:
  11.0 62.9 all-gather.6
  77.0 52.9 all-gather.8
  131.5 36.3 all-gather.10
  226.7 37.8 all-gather.12
  327.4 48.9 reduce-scatter.12
  380.6 49.0 reduce-scatter.10
  516.1 109.8 reduce-scatter.8
  633.3 118.1 reduce-scatter.6
where the time goes:
time: 768 us; the launch traced here: 759 us
  matrix products  238 us (31%)
  waiting for transfers between devices  194 us (25%)
  blocking collectives  171 us (22%)
  other arithmetic  69.5 us (9%)
  local copies, waits for them, and re-layouts  52.9 us (7%)
  starting transfers between devices  17.7 us (2%)
  between operations  16.3 us (2%)
    reduce_scatter x1, waiting for transfers between devices, shards(): lax.psum_scatter(grad_attn_in, ('dp', 'expert'), scatter_dimension=0, til...  88.4 us
    dot_general x6, matrix products, product(): return jnp.dot(left, right, preferred_element_type=jnp.float32)  71.8 us
    dot_general x12, matrix products, contract(): lax.dot_general(left, right, (((left_dim,), (right_dim,)), ((), ())), pre...  70.7 us
    all_gather x1, blocking collectives, shards(): lax.all_gather(ln_gain, ('dp', 'expert'), axis=1, tiled=True)  69.6 us
    all_gather x1, blocking collectives, shards(): lax.all_gather(ln_bias, ('dp', 'expert'), axis=1, tiled=True)  63.2 us
    all_to_all x1, waiting for transfers between devices, shards(): lax.all_to_all(result, 'expert', split_axis=0, concat_axis=0, tiled=True)  47.3 us
    unnamed x1, blocking collectives  38.2 us
    dot_general x2, matrix products, shards(): jnp.einsum('qhd,khd->hqk', grad_block, value_rows[:last_row], preferred_e...  32.4 us
  transfers between devices with their start and end apart: 12, of which 4 were waited for; matrix products, arithmetic and copies ran while one was open for 46% of the time, Pallas kernels for 0%

commit v1 on v0

--- a/solution.py
+++ b/solution.py
@@ -7,6 +7,28 @@
 HEAD_DIM = 64
 eps = 1e-05
 masked_score = -1e30
+
+
+def in_order(blocks, dim):
+    blocks = jnp.moveaxis(blocks, 0, dim)
+    shape = blocks.shape
+    return blocks.reshape(*shape[:dim], shape[dim] * shape[dim + 1], *shape[dim + 2 :])
+
+
+def doubled(x, axis):
+    length = lax.axis_size(axis)
+    blocks = x[None]
+    for level in range(length.bit_length() - 1):
+        bit = 1 << level
+        other = lax.ppermute(blocks, axis, [(i, i ^ bit) for i in range(length)])
+        both = jnp.stack([blocks, other])
+        upper = lax.axis_index(axis) >> level & 1
+        blocks = jnp.where(upper == 0, both, both[::-1]).reshape(-1, *x.shape)
+    return blocks
+
+
+def gather_by_bits(x, axis, dim):
+    return in_order(doubled(x, axis), dim)
 
 
 def product(left, right):
@@ -53,7 +75,7 @@
     all_in, all_out, gains, shifts = (
         lax.all_gather(attn_in, ("dp", "expert"), axis=0, tiled=True),
         lax.all_gather(attn_out, ("dp", "expert"), axis=0, tiled=True),
-        lax.all_gather(ln_gain, ("dp", "expert"), axis=1, tiled=True),
+        gather_by_bits(ln_gain, ("dp", "expert"), 1),
         lax.all_gather(ln_bias, ("dp", "expert"), axis=1, tiled=True),
     )
     gains = gains.astype(jnp.float32)

time: 768 us -> 703 us (0.915)
  blocking collectives: 171 us -> 106 us
  matrix products: 238 us -> 230 us
    all_gather x1 -> x0, blocking collectives: 69.6 us -> none  [shards(): lax.all_gather(ln_gain, ('dp', 'expert'), axis=1, tiled=True)]
    dot_general x6, matrix products: 71.8 us -> 63.5 us  [product(): return jnp.dot(left, right, preferred_element_type=jnp.float32)]
    ppermute x0 -> x5, starting transfers between devices: none -> 7.95 us  [doubled(): other = lax.ppermute(blocks, axis, [(i, i ^ bit) for i in range(length)])]
    unnamed x168 -> x172, local copies, waits for them, and re-layouts: 20.7 us -> 20.1 us
  transfers between devices with their start and end apart: 12 -> 17, of which waited for: 4 -> 8; matrix products, arithmetic and copies ran while one was open for 46% -> 49% of each run, Pallas kernels for 0% -> 0%
where the time goes in v1:
time: 703 us; the launch traced here: 697 us
  matrix products  230 us (33%)
  waiting for transfers between devices  198 us (28%)
  blocking collectives  106 us (15%)
  other arithmetic  69.8 us (10%)
  local copies, waits for them, and re-layouts  52.2 us (7%)
  starting transfers between devices  25.1 us (4%)
  between operations  16.5 us (2%)
    reduce_scatter x1, waiting for transfers between devices, shards(): lax.psum_scatter(grad_attn_in, ('dp', 'expert'), scatter_dimension=0, til...  88.1 us
    dot_general x12, matrix products, contract(): lax.dot_general(left, right, (((left_dim,), (right_dim,)), ((), ())), pre...  70.8 us
    all_gather x1, blocking collectives, shards(): lax.all_gather(ln_bias, ('dp', 'expert'), axis=1, tiled=True)  67.6 us
    dot_general x6, matrix products, product(): return jnp.dot(left, right, preferred_element_type=jnp.float32)  63.5 us
    all_to_all x1, waiting for transfers between devices, shards(): lax.all_to_all(result, 'expert', split_axis=0, concat_axis=0, tiled=True)  47.2 us
    unnamed x1, blocking collectives  38.3 us
    dot_general x2, matrix products, shards(): jnp.einsum('qhd,khd->hqk', grad_block, value_rows[:last_row], preferred_e...  32.5 us
    all_to_all x1, waiting for transfers between devices, shards(): lax.all_to_all(send_rows.reshape(experts, capacity, model_width), 'expert...  29.8 us
  transfers between devices with their start and end apart: 17, of which 8 were waited for; matrix products, arithmetic and copies ran while one was open for 49% of the time, Pallas kernels for 0%

profile of v1, /device:TPU:0, one launch (start us, length us, event | category | flops | bytes accessed | tf_op | source)
XLA Modules:
  0.0 697.0 jit_solution(14265627279458918408)
XLA Ops:
  29.0 67.6 %all-gather = bf16[32,24,2]{1,2,0:T(2,128)(2,1)S(1)} all-gather(bf16[1,24,2]{1,2,0:T(2,128)(2,1)S(1)} %bitcast.211), channel_id=1, replica_groups=mesh['dp'=4,'expert'=8] {'dp','expert'}, dimensions={0}, use_global_device_ids=true | all-gather | bytes 3168 | tf_op jit(solution)/shard_map/all_gather | solution.py:79
  108.6 11.1 %fusion.14 = (f32[12,512]{1,0:T(8,128)S(1)}, f32[12,512,1024]{2,1,0:T(8,128)}) fusion(pred[512,1024]{1,0:T(8,128)(4,1)S(1)} %fusion.50, bf16[512,12,64]{0,2,1:T(8,128)(2,1)S(1)} %bitcast.173, bf16[1024,12,64]{0,2,1:T(8,128)(2,1)S(1)} %bitcast.171), kind=kOutput, calls=%fused_computation.40 | convolution fusion | flops 824174592 | bytes 28073984 | tf_op jit(solution)/shard_map/qhd,khd->hqk/dot_general | solution.py:64
  119.7 12.4 %fusion = f32[12,512]{1,0:T(8,128)S(1)} fusion(f32[12,512]{1,0:T(8,128)S(1)} %get-tuple-element.139, f32[12,512,1024]{2,1,0:T(8,128)} %get-tuple-element.140, pred[512,1024]{1,0:T(8,128)(4,1)S(1)} %fusion.50), kind=kLoop, calls=%fused_computation.10 | loop fusion | flops 25159680 | bytes 25739264 | tf_op jit(solution)/shard_map/reduce_sum | solution.py:103
  135.8 8.5 %fusion.59 = bf16[512,12,64]{0,2,1:T(8,128)(2,1)} fusion(bf16[1024,12,64]{0,2,1:T(8,128)(2,1)S(1)} %bitcast.177, f32[12,512]{1,0:T(8,128)S(1)} %fusion, f32[12,512]{1,0:T(8,128)S(1)} %get-tuple-element.139, f32[12,512,1024]{2,1,0:T(8,128)S(1)} %copy-done, pred[512,1024]{1,0:T(8,128)(4,1)S(1)} %fusion.50), kind=kOutput, calls=%fused_computation.105 | convolution fusion | flops 837156864 | bytes 28098560 | tf_op jit(solution)/shard_map/hqk,khd->qhd/dot_general | solution.py:107
  163.9 6.6 scatter_custom_fusion
  174.6 7.1 %scatter_custom_fusion.1 = bf16[1152,768]{1,0:T(8,128)(2,1)} fusion(s32[1024]{0:T(1024)S(1)} %get-tuple-element.132, bf16[1024,768]{1,0:T(8,128)(2,1)} %param.31, bf16[]{:T(256)} %constant.201.clone.1), kind=kCustom, calls=%fused_computation.118 | custom fusion | bytes 1769984 | tf_op jit(solution)/shard_map/scatter | solution.py:147
  181.7 29.8 %all-to-all-done = bf16[8,144,768]{2,1,0:T(8,128)(2,1)S(1)} async-done(((bf16[8,144,768]{2,1,0:T(8,128)(2,1)}), bf16[8,144,768]{2,1,0:T(8,128)(2,1)S(1)}, u32[]{:S(2)}, u32[]{:S(2)}) %all-to-all-start) | async-done | bytes 1769504 | tf_op jit(solution)/shard_map/all_to_all | solution.py:125
  215.9 39.8 %multiply_convert_fusion.1 = (bf16[1152,3072]{1,0:T(8,128)(2,1)}, f32[1152,3072]{1,0:T(8,128)}, f32[1152,3072]{1,0:T(8,128)}) fusion(bf16[1152,768]{1,0:T(8,128)(2,1)S(1)} %bitcast.189, bf16[1,768,3072]{2,1,0:T(8,128)(2,1)} %all-gather.10.cloned.1.call-done), kind=kOutput, calls=%fused_computation.15 | convolution fusion | flops 5665849344 | bytes 41877504 | tf_op jit(solution)/shard_map/dot_general | solution.py:35
  256.0 10.6 %fusion.31 = bf16[1,3072,768]{2,1,0:T(8,128)(2,1)} fusion(bf16[1152,3072]{1,0:T(8,128)(2,1)} %get-tuple-element.121, bf16[1152,768]{1,0:T(8,128)(2,1)} %bitcast.40), kind=kOutput, calls=%fused_computation.64 | convolution fusion | flops 5438177280 | bytes 13565952 | tf_op jit(solution)/shard_map/dot_general | solution.py:39
  266.6 20.4 %add_convert_fusion = bf16[1152,3072]{1,0:T(8,128)(2,1)} fusion(f32[1152,3072]{1,0:T(8,128)} %get-tuple-element.122, bf16[1152,768]{1,0:T(8,128)(2,1)} %bitcast.40, f32[1152,3072]{1,0:T(8,128)} %get-tuple-element.145, bf16[1,3072,768]{2,1,0:T(8,128)(2,1)} %all-gather.12.cloned.1.call-done), kind=kOutput, calls=%fused_computation.14 | convolution fusion | flops 5485363200 | bytes 41877504 | tf_op jit(solution)/shard_map/dot_general | solution.py:39
  287.1 10.6 %fusion.35 = bf16[1152,768]{1,0:T(8,128)(2,1)} fusion(bf16[1152,3072]{1,0:T(8,128)(2,1)} %add_convert_fusion, bf16[1,768,3072]{2,1,0:T(8,128)(2,1)} %all-gather.10.cloned.1.call-done), kind=kOutput, calls=%fused_computation.68 | convolution fusion | flops 5436702720 | bytes 13565952 | tf_op jit(solution)/shard_map/dot_general | solution.py:39
  308.5 11.0 %fusion.30 = bf16[1,768,3072]{2,1,0:T(8,128)(2,1)} fusion(bf16[1152,768]{1,0:T(8,128)(2,1)S(1)} %bitcast.190, bf16[1152,3072]{1,0:T(8,128)(2,1)} %add_convert_fusion), kind=kOutput, calls=%fused_computation.63 | convolution fusion | flops 5438177280 | bytes 13565952 | tf_op jit(solution)/shard_map/dot_general | solution.py:39
  319.5 23.0 %all-to-all-done.3 = bf16[8,144,768]{2,1,0:T(8,128)(2,1)S(1)} async-done(((bf16[8,144,768]{2,1,0:T(8,128)(2,1)}), bf16[8,144,768]{2,1,0:T(8,128)(2,1)S(1)}, u32[]{:S(2)}, u32[]{:S(2)}) %all-to-all-start.3) | async-done | bytes 1769504 | tf_op jit(solution)/shard_map/all_to_all | solution.py:174
  364.2 10.9 %multiply_reduce_fusion.1 = (f32[12,512]{1,0:T(8,128)S(1)}, f32[12,512,512]{1,2,0:T(8,128)}) fusion(f32[12,512]{1,0:T(8,128)S(1)} %copy-done.47, f32[12,512,512]{1,2,0:T(8,128)} %copy-done.1, pred[512,512]{0,1:T(8,128)(4,1)S(1)} %copy-done.24, bf16[512,12,64]{0,2,1:T(8,128)(2,1)S(1)} %bitcast.181, bf16[512,12,64]{0,2,1:T(8,128)(2,1)S(1)} %bitcast.180), kind=kOutput, calls=%fused_computation.32 | convolution fusion | flops 418375680 | bytes 27049984 | tf_op jit(solution)/shard_map/qhd,khd->hqk/dot_general | solution.py:195
  375.4 7.0 %multiply_convert_fusion.2 = bf16[12,512,512]{1,2,0:T(8,128)(2,1)S(1)} fusion(f32[12,512,512]{1,2,0:T(8,128)} %get-tuple-element.149, f32[12,512]{1,0:T(8,128)S(1)} %get-tuple-element.148, f32[12,512]{1,0:T(8,128)S(1)} %copy-done.47, f32[12,512,512]{1,2,0:T(8,128)S(1)} %bitcast.162, pred[512,512]{0,1:T(8,128)(4,1)S(1)} %copy-done.24), kind=kLoop, calls=%fused_computation.31 | loop fusion | flops 18874368 | bytes 31768576 | tf_op jit(solution)/shard_map/convert_element_type | solution.py:199
  385.6 21.6 %multiply_reduce_fusion = (f32[12,512]{1,0:T(8,128)S(1)}, f32[12,512,1024]{2,1,0:T(8,128)}) fusion(f32[12,512]{1,0:T(8,128)S(1)} %copy-done.46, f32[12,512,1024]{2,1,0:T(8,128)} %get-tuple-element.140, pred[512,1024]{1,0:T(8,128)(4,1)S(1)} %copy-done.15, bf16[512,12,64]{0,2,1:T(8,128)(2,1)S(1)} %bitcast.183, bf16[1024,12,64]{0,2,1:T(8,128)(2,1)S(1)} %bitcast.178), kind=kOutput, calls=%fused_computation.5 | convolution fusion | flops 836757504 | bytes 53264384 | tf_op jit(solution)/shard_map/qhd,khd->hqk/dot_general | solution.py:195
  407.2 17.2 %multiply_convert_fusion = bf16[12,512,1024]{2,1,0:T(8,128)(2,1)S(1)} fusion(f32[12,512,1024]{2,1,0:T(8,128)} %get-tuple-element.147, f32[12,512]{1,0:T(8,128)S(1)} %get-tuple-element.146, f32[12,512]{1,0:T(8,128)S(1)} %copy-done.46, f32[12,512,1024]{2,1,0:T(8,128)} %get-tuple-element.140, pred[512,1024]{1,0:T(8,128)(4,1)} %copy-done.14), kind=kLoop, calls=%fused_computation.4 | loop fusion | flops 37748736 | bytes 63488000 | tf_op jit(solution)/shard_map/convert_element_type | solution.py:199
  424.4 7.4 %multiply_convert_fusion.3 = bf16[12,64,512]{2,1,0:T(8,128)(2,1)} fusion(bf16[1024,12,64]{0,2,1:T(8,128)(2,1)} %bitcast.172, bf16[12,512,1024]{2,1,0:T(8,128)(2,1)S(1)} %multiply_convert_fusion), kind=kOutput, calls=%fused_computation.100 | convolution fusion | flops 806092800 | bytes 14942208 | tf_op jit(solution)/shard_map/hqk,khd->qhd/dot_general | solution.py:201
  431.8 9.1 %fusion.54 = f32[512,12,64]{0,2,1:T(8,128)} fusion(bf16[512,12,64]{0,2,1:T(8,128)(2,1)} %bitcast.182, f32[12,512]{1,0:T(8,128)S(1)} %copy-done.47, f32[12,512,512]{1,2,0:T(8,128)} %copy-done.1, pred[512,512]{0,1:T(8,128)(4,1)S(1)} %copy-done.24), kind=kOutput, calls=%fused_computation.102 | convolution fusion | flops 415236096 | bytes 15228928 | tf_op jit(solution)/shard_map/hqk,qhd->khd/dot_general | solution.py:216
  441.0 13.5 %fusion.46 = bf16[1024,12,64]{0,2,1:T(8,128)(2,1)} fusion(f32[512,12,64]{0,2,1:T(8,128)} %fusion.54, bf16[512,12,64]{0,2,1:T(8,128)(2,1)S(1)} %bitcast.184, f32[12,512]{1,0:T(8,128)S(1)} %copy-done.46, f32[12,512,1024]{2,1,0:T(8,128)} %get-tuple-element.140, pred[512,1024]{1,0:T(8,128)(4,1)S(1)} %copy-done.16), kind=kOutput, calls=%fused_computation.76 | convolution fusion | flops 832045056 | bytes 29646848 | tf_op jit(solution)/shard_map/hqk,qhd->khd/dot_general | solution.py:216
  471.8 10.3 %fusion.38 = bf16[1152,768]{1,0:T(8,128)(2,1)} fusion(bf16[1152,3072]{1,0:T(8,128)(2,1)} %get-tuple-element.121, bf16[1,3072,768]{2,1,0:T(8,128)(2,1)} %all-gather.12.cloned.1.call-done), kind=kOutput, calls=%fused_computation.69 | convolution fusion | flops 5436702720 | bytes 13565952 | tf_op jit(solution)/shard_map/dot_general | solution.py:35
  485.6 47.2 %all-to-all-done.1 = bf16[8,144,768]{2,1,0:T(8,128)(2,1)S(1)} async-done(((bf16[8,144,768]{2,1,0:T(8,128)(2,1)}), bf16[8,144,768]{2,1,0:T(8,128)(2,1)S(1)}, u32[]{:S(2)}, u32[]{:S(2)}) %all-to-all-start.1) | async-done | bytes 1769504 | tf_op jit(solution)/shard_map/all_to_all | solution.py:142
  556.4 38.3 %all-reduce.4 = (f32[2,768]{1,0:T(2,128)S(1)}, f32[2,768]{1,0:T(2,128)S(1)}) all-reduce(f32[2,768]{1,0:T(2,128)S(1)} %get-tuple-element.151, f32[2,768]{1,0:T(2,128)S(1)} %get-tuple-element.152), channel_id=4, replica_groups=mesh['dp'=4,'expert'=8] {'dp','expert'}, use_global_device_ids=true, to_apply=%region_23.24.clone | all-reduce | flops 3072 | bytes 24576
  601.7 88.1 %reduce-scatter.7.cloned.1.call-done = f32[72,768]{1,0:T(8,128)} async-done(((f32[2304,768]{1,0:T(8,128)}), f32[72,768]{1,0:T(8,128)}) %reduce-scatter.7.cloned.1.call-update) | async-done | bytes 221200 | tf_op jit(solution)/shard_map/reduce_scatter | solution.py:244
  (301 shorter events, 151.4 us)
Async XLA Ops:
  7.2 93.8 %all-gather.6.cloned.1.call-start = ((), (), s32[]{:S(2)}) async-start(), calls=%async_computation.8 | async-start | bytes 3649536 | tf_op jit(solution)/shard_map/all_gather | solution.py:76
  7.9 149.8 %all-gather.8.cloned.1.call-start = ((), (), s32[]{:S(2)}) async-start(), calls=%async_computation.9 | async-start | bytes 1216512 | tf_op jit(solution)/shard_map/all_gather | solution.py:77
  8.7 207.2 %all-gather.10.cloned.1.call-start = ((), (), s32[]{:S(2)}) async-start(), calls=%async_computation.10 | async-start | bytes 5898240 | tf_op jit(solution)/shard_map/all_gather | solution.py:133
  8.7 11.9 %collective-permute-start = (bf16[1,2,24]{2,1,0:T(2,128)(2,1)}, bf16[1,2,24]{2,1,0:T(2,128)(2,1)S(1)}, u32[]{:S(2)}, u32[]{:S(2)}) collective-permute-start(bf16[1,2,24]{2,1,0:T(2,128)(2,1)} %bitcast.212), channel_id=1, source_target_pairs={{0,1},{1,0},{2,3},{3,2},{4,5},{5,4},{6,7},{7,6},{8,9},{9,8},{10,11... | collective-permute-start | bytes 296 | tf_op jit(solution)/shard_map/ppermute | solution.py:23
  16.1 135.9 %copy-start.23 = (pred[512,512]{0,1:T(8,128)(4,1)}, pred[512,512]{0,1:T(8,128)(4,1)S(1)}, u32[]{:S(2)}) copy-start(pred[512,512]{0,1:T(8,128)(4,1)S(1)} %fusion.61) | copy-start | bytes 786436
  17.2 118.5 %copy-start.14 = (pred[512,1024]{1,0:T(8,128)(4,1)}, pred[512,1024]{1,0:T(8,128)(4,1)S(1)}, u32[]{:S(2)}) copy-start(pred[512,1024]{1,0:T(8,128)(4,1)S(1)} %fusion.50) | copy-start | bytes 1572868
  19.2 138.5 %copy-start.7 = (bf16[1024,768]{0,1:T(8,128)(2,1)}, bf16[1024,768]{0,1:T(8,128)(2,1)S(1)}, u32[]{:S(2)}) copy-start(bf16[1024,768]{0,1:T(8,128)(2,1)S(1)} %copy.66) | copy-start | bytes 4718596
  19.5 112.6 %copy-start.54 = (f32[1024]{0:T(1024)}, f32[1024]{0:T(1024)S(1)}, u32[]{:S(2)}) copy-start(f32[1024]{0:T(1024)S(1)} %broadcast_multiply_fusion.1) | copy-start | bytes 12292
  20.0 80.7 %copy-start.60 = (f32[1024]{0:T(1024)}, f32[1024]{0:T(1024)S(1)}, u32[]{:S(2)}) copy-start(f32[1024]{0:T(1024)S(1)} %fusion.44) | copy-start | bytes 12292
  20.6 3.6 collective-permute-start.1
  24.3 4.6 collective-permute-start.2
  26.9 105.2 %copy-start.65 = (f32[1024]{0:T(1024)}, f32[1024]{0:T(1024)S(1)}, u32[]{:S(2)}) copy-start(f32[1024]{0:T(1024)S(1)} %fusion.82) | copy-start | bytes 12292
  28.9 68.0 %collective-permute-start.3 = (bf16[8,2,24]{2,1,0:T(2,128)(2,1)S(1)}, bf16[8,2,24]{2,1,0:T(2,128)(2,1)S(1)}, u32[]{:S(2)}, u32[]{:S(2)}) collective-permute-start(bf16[8,2,24]{2,1,0:T(2,128)(2,1)S(1)} %bitcast.203), channel_id=1, source_target_pairs={{0,8},{1,9},{2,10},{3,11},{4,12},{5,13},{6,14},{7,15},{8,0},{9,1},... | collective-permute-start | bytes 2312 | tf_op jit(solution)/shard_map/ppermute | solution.py:23
  96.9 3.7 collective-permute-start.4
  100.8 60.6 %copy-start.50 = (f32[768]{0:T(1024)}, f32[768]{0:T(1024)S(1)}, u32[]{:S(2)}) copy-start(f32[768]{0:T(1024)S(1)} %mul.230) | copy-start | bytes 9220
  170.4 41.1 %all-to-all-start = ((bf16[8,144,768]{2,1,0:T(8,128)(2,1)}), bf16[8,144,768]{2,1,0:T(8,128)(2,1)S(1)}, u32[]{:S(2)}, u32[]{:S(2)}) async-start(bf16[8,144,768]{2,1,0:T(8,128)(2,1)} %bitcast.33), calls=%async_computation | async-start | bytes 3538944 | tf_op jit(solution)/shard_map/all_to_all | solution.py:125
  174.0 92.6 %all-gather.12.cloned.1.call-start = ((), (), s32[]{:S(2)}) async-start(), calls=%async_computation.11 | async-start | bytes 5898240 | tf_op jit(solution)/shard_map/all_gather | solution.py:134
  211.5 44.5 %all-to-all-start.2 = ((bf16[8,144,768]{2,1,0:T(8,128)(2,1)}), bf16[8,144,768]{2,1,0:T(8,128)(2,1)}, u32[]{:S(2)}, u32[]{:S(2)}) async-start(bf16[8,144,768]{2,1,0:T(8,128)(2,1)} %bitcast.39), calls=%async_computation.2 | async-start | bytes 3538944 | tf_op jit(solution)/shard_map/all_to_all | solution.py:149
  215.8 380.1 %reduce-scatter.13.cloned.1.call-start = ((), (), s32[]{:S(2)}) async-start(), calls=%async_computation.15 | async-start | bytes 5898240 | tf_op jit(solution)/shard_map/reduce_scatter | solution.py:170
  297.7 44.9 %all-to-all-start.3 = ((bf16[8,144,768]{2,1,0:T(8,128)(2,1)}), bf16[8,144,768]{2,1,0:T(8,128)(2,1)S(1)}, u32[]{:S(2)}, u32[]{:S(2)}) async-start(bf16[8,144,768]{2,1,0:T(8,128)(2,1)} %bitcast.191), calls=%async_computation.3 | async-start | bytes 3538944 | tf_op jit(solution)/shard_map/all_to_all | solution.py:174
  303.1 295.7 %reduce-scatter.11.cloned.1.call-start = ((), (), s32[]{:S(2)}) async-start(), calls=%async_computation.14 | async-start | bytes 5898240 | tf_op jit(solution)/shard_map/reduce_scatter | solution.py:167
  319.5 282.2 %reduce-scatter.9.cloned.1.call-start = ((), (), s32[]{:S(2)}) async-start(), calls=%async_computation.13 | async-start | bytes 2433024 | tf_op jit(solution)/shard_map/reduce_scatter | solution.py:245
  454.5 235.3 %reduce-scatter.7.cloned.1.call-start = ((), (), s32[]{:S(2)}) async-start(), calls=%async_computation.12 | async-start | bytes 7299072 | tf_op jit(solution)/shard_map/reduce_scatter | solution.py:244
  482.0 50.9 %all-to-all-start.1 = ((bf16[8,144,768]{2,1,0:T(8,128)(2,1)}), bf16[8,144,768]{2,1,0:T(8,128)(2,1)S(1)}, u32[]{:S(2)}, u32[]{:S(2)}) async-start(bf16[8,144,768]{2,1,0:T(8,128)(2,1)} %bitcast.37), calls=%async_computation.1 | async-start | bytes 3538944 | tf_op jit(solution)/shard_map/all_to_all | solution.py:142
  (76 other events, 525.8 us)
Sparse Core Ops, SparseCore 0:
  11.0 62.9 all-gather.5
  77.0 52.9 all-gather.7
  131.5 36.3 all-gather.9
  176.1 37.8 all-gather.11
  266.7 48.4 reduce-scatter.12
  319.6 48.8 reduce-scatter.10
  454.6 109.7 reduce-scatter.8
  571.6 118.0 reduce-scatter.6
